TPU v7x, 128 devices: a whole 4x4x4 slice. The times are simulated.
128 devices in a mesh: occ: 8 (over y, core), vir: 16 (over z, x).
Axes of the slice: x: 4, y: 4, z: 4, core: 2. Of those that a mesh axis runs over, the one named last changes fastest.
Arguments:
- amplitudes: bfloat16 [9216, 16384], P('occ', 'vir'), may hold values from -6 to 6
- integrals: bfloat16 [16, 8, 1024, 1024], P('vir'), may hold values from -0.0625 to 0.0625
- cd_tiles: int32 [16, 8], P('vir'), may hold values from 0 to 15, as said below
- cd_count: int32 [16], P('vir'), may hold values from 1 to 8, as said below
Outputs:
- residual: bfloat16 [9216, 16384], P('occ', 'vir')
Inputs may be any that keep to these rules, and one draw needn't show every extreme that they name: `cd_tiles`: entries of one row are distinct and the first is the row's own pair tile. `cd_count`: slots at or past the count are unused.
All inputs are finite; a program needn't handle non-finite values.
Results may differ from a plain program's by a relative error of at most 0.0075.
Values may be sent and summed in bfloat16 or wider, within the bound.
No kernel may reach another device: no remote copies, remote signals or barrier semaphores. Data moves between devices by JAX's collectives and lax.ppermute only.
A program may use at most 128 MiB of HBM per device.

v0:
```python
import jax
import jax.numpy as jnp
from jax import lax
from jax.sharding import PartitionSpec as P

TW = 32
K = 1024
OCC_DEV = 12
CD_MAX = 8


def swapped(shard, axis, apart):
    return lax.ppermute(shard, axis, [(i, i ^ 1 << apart) for i in range(lax.axis_size(axis))])


def reflect_rows(matrix):
    occ_devices = lax.axis_size("occ")
    reshaped = matrix.reshape(OCC_DEV, occ_devices, OCC_DEV, matrix.shape[1])
    arrived = lax.all_to_all(reshaped, "occ", split_axis=1, concat_axis=1, tiled=True)
    return arrived.transpose(2, 1, 0, 3).reshape(matrix.shape)


def reflect_tiles(matrix):
    arrived = swapped(matrix, "vir", 0)
    row_count = matrix.shape[0]
    return arrived.reshape(row_count, TW, TW).transpose(0, 2, 1).reshape(row_count, K)


def on_device(amplitudes, integrals, cd_tiles, cd_count):
    row_count = amplitudes.shape[0]
    listed = cd_tiles[0]
    live_count = cd_count[0]
    blocks = integrals[0]
    zero_block = jnp.zeros((row_count, K), jnp.float32)

    def product(col_tile, slot_index):
        int_block = lax.dynamic_index_in_dim(blocks, slot_index, 0, keepdims=False)
        return lax.dot_general(
            col_tile, int_block, (((1,), (1,)), ((), ())), preferred_element_type=jnp.float32
        )

    gathered = lax.all_gather(amplitudes, "vir", axis=1, tiled=True)

    def visit_slot(slot_pos, running):
        tile_id = listed[slot_pos]

        def apply_block(current):
            col_tile = lax.dynamic_slice_in_dim(gathered, tile_id * K, K, 1)
            return current + product(col_tile, slot_pos)

        return lax.cond(slot_pos < live_count, apply_block, lambda current: current, running)

    ladder = lax.fori_loop(0, CD_MAX, visit_slot, zero_block)
    ladder = ladder.astype(jnp.bfloat16)
    mirrored = reflect_tiles(reflect_rows(ladder))
    summed = ladder.astype(jnp.float32) + mirrored.astype(jnp.float32)
    return summed.astype(jnp.bfloat16)


def solution(mesh):
    placed = (P("occ", "vir"), P("vir", None, None, None), P("vir", None), P("vir"))
    return jax.shard_map(
        on_device, mesh=mesh, in_specs=placed, out_specs=P("occ", "vir"), check_vma=False
    )
```

profile of v0, /device:TPU:6, one launch (start us, length us, event | category | flops | bytes accessed | tf_op | source)
XLA Modules:
  0.0 456.2 jit_solution(4664653060656685572)
XLA Ops:
  6.5 0.7 all-gather.2.cloned.1.call-update
  7.3 223.1 %all-gather.2.cloned.1.call-done = bf16[1152,16384]{1,0:T(8,128)(2,1)} async-done(((bf16[1152,1024]{1,0:T(8,128)(2,1)}), bf16[1152,16384]{1,0:T(8,128)(2,1)}) %all-gather.2.cloned.1.call-update) | async-done | bytes 37748752 | tf_op jit(solution)/shard_map/all_gather | solution.py:42
  230.4 2.8 broadcast_in_dim.3
  233.1 83.6 %while.16 = (s32[]{:T(128)}, f32[1152,1024]{1,0:T(8,128)}, s32[]{:T(128)}, s32[8]{0:T(128)S(1)}, bf16[1152,16384]{1,0:T(8,128)(2,1)}, /*index=5*/bf16[8,1024,1024]{2,1,0:T(8,128)(2,1)}, s32[]{:T(128)}) while((s32[]{:T(128)}, f32[1152,1024]{1,0:T(8,128)}, s32[]{:T(128)}, s32[8]{0:T(128)S(1)}, bf16[1152,16384]{1,0:T(8,128)(2,1)}, ...), condition=%wide.region_3.4_spmd, body=%wide.region_0.3_spmd.sunk | while | flops 2417098752 | bytes 13893871 | solution.py:53
  233.8 9.8 %conditional.2 = (f32[1152,1024]{1,0:T(8,128)}) conditional(s32[]{:T(128)} %convert_element_type.41, f32[1152,1024]{1,0:T(8,128)} %get-tuple-element.236, (s32[]{:T(128)}, s32[8]{0:T(128)S(1)}, bf16[1152,16384]{1,0:T(8,128)(2,1)}, bf16[8,1024,1024]{2,1,0:T(8,128)(2,1)}, f32[1152,1024]{1,0:T(8,128)}) %tuple.45), branch_computations={%region_1.0_spmd, %region_2.2_spmd} | conditional | flops 2417098752 | bytes 13893740 | solution.py:51
  235.1 8.5 %convolution_add_fusion = f32[1152,1024]{1,0:T(8,128)} fusion(f32[1152,1024]{1,0:T(8,128)} %get-tuple-element.165, bf16[1152,16384]{1,0:T(8,128)(2,1)} %get-tuple-element.166, s32[]{:T(128)S(6)} %select_n.19, bf16[8,1024,1024]{2,1,0:T(8,128)(2,1)} %get-tuple-element.169, s32[]{:T(128)S(6)} %select_n.18), kind=kOutput, calls=%fused_computation | convolution fusion | flops 2417098752 | bytes 13893640 | tf_op jit(solution)/shard_map/while/body/eval_jaxpr/cond/branch_1_fun/dot_general | solution.py:38
  244.2 9.8 %conditional.2 = (f32[1152,1024]{1,0:T(8,128)}) conditional(s32[]{:T(128)} %convert_element_type.41, f32[1152,1024]{1,0:T(8,128)} %get-tuple-element.236, (s32[]{:T(128)}, s32[8]{0:T(128)S(1)}, bf16[1152,16384]{1,0:T(8,128)(2,1)}, bf16[8,1024,1024]{2,1,0:T(8,128)(2,1)}, f32[1152,1024]{1,0:T(8,128)}) %tuple.45), branch_computations={%region_1.0_spmd, %region_2.2_spmd} | conditional | flops 2417098752 | bytes 13893740 | solution.py:51
  245.5 8.5 %convolution_add_fusion = f32[1152,1024]{1,0:T(8,128)} fusion(f32[1152,1024]{1,0:T(8,128)} %get-tuple-element.165, bf16[1152,16384]{1,0:T(8,128)(2,1)} %get-tuple-element.166, s32[]{:T(128)S(6)} %select_n.19, bf16[8,1024,1024]{2,1,0:T(8,128)(2,1)} %get-tuple-element.169, s32[]{:T(128)S(6)} %select_n.18), kind=kOutput, calls=%fused_computation | convolution fusion | flops 2417098752 | bytes 13893640 | tf_op jit(solution)/shard_map/while/body/eval_jaxpr/cond/branch_1_fun/dot_general | solution.py:38
  254.7 9.8 %conditional.2 = (f32[1152,1024]{1,0:T(8,128)}) conditional(s32[]{:T(128)} %convert_element_type.41, f32[1152,1024]{1,0:T(8,128)} %get-tuple-element.236, (s32[]{:T(128)}, s32[8]{0:T(128)S(1)}, bf16[1152,16384]{1,0:T(8,128)(2,1)}, bf16[8,1024,1024]{2,1,0:T(8,128)(2,1)}, f32[1152,1024]{1,0:T(8,128)}) %tuple.45), branch_computations={%region_1.0_spmd, %region_2.2_spmd} | conditional | flops 2417098752 | bytes 13893740 | solution.py:51
  256.0 8.5 %convolution_add_fusion = f32[1152,1024]{1,0:T(8,128)} fusion(f32[1152,1024]{1,0:T(8,128)} %get-tuple-element.165, bf16[1152,16384]{1,0:T(8,128)(2,1)} %get-tuple-element.166, s32[]{:T(128)S(6)} %select_n.19, bf16[8,1024,1024]{2,1,0:T(8,128)(2,1)} %get-tuple-element.169, s32[]{:T(128)S(6)} %select_n.18), kind=kOutput, calls=%fused_computation | convolution fusion | flops 2417098752 | bytes 13893640 | tf_op jit(solution)/shard_map/while/body/eval_jaxpr/cond/branch_1_fun/dot_general | solution.py:38
  265.1 9.8 %conditional.2 = (f32[1152,1024]{1,0:T(8,128)}) conditional(s32[]{:T(128)} %convert_element_type.41, f32[1152,1024]{1,0:T(8,128)} %get-tuple-element.236, (s32[]{:T(128)}, s32[8]{0:T(128)S(1)}, bf16[1152,16384]{1,0:T(8,128)(2,1)}, bf16[8,1024,1024]{2,1,0:T(8,128)(2,1)}, f32[1152,1024]{1,0:T(8,128)}) %tuple.45), branch_computations={%region_1.0_spmd, %region_2.2_spmd} | conditional | flops 2417098752 | bytes 13893740 | solution.py:51
  266.4 8.5 %convolution_add_fusion = f32[1152,1024]{1,0:T(8,128)} fusion(f32[1152,1024]{1,0:T(8,128)} %get-tuple-element.165, bf16[1152,16384]{1,0:T(8,128)(2,1)} %get-tuple-element.166, s32[]{:T(128)S(6)} %select_n.19, bf16[8,1024,1024]{2,1,0:T(8,128)(2,1)} %get-tuple-element.169, s32[]{:T(128)S(6)} %select_n.18), kind=kOutput, calls=%fused_computation | convolution fusion | flops 2417098752 | bytes 13893640 | tf_op jit(solution)/shard_map/while/body/eval_jaxpr/cond/branch_1_fun/dot_general | solution.py:38
  275.6 9.8 %conditional.2 = (f32[1152,1024]{1,0:T(8,128)}) conditional(s32[]{:T(128)} %convert_element_type.41, f32[1152,1024]{1,0:T(8,128)} %get-tuple-element.236, (s32[]{:T(128)}, s32[8]{0:T(128)S(1)}, bf16[1152,16384]{1,0:T(8,128)(2,1)}, bf16[8,1024,1024]{2,1,0:T(8,128)(2,1)}, f32[1152,1024]{1,0:T(8,128)}) %tuple.45), branch_computations={%region_1.0_spmd, %region_2.2_spmd} | conditional | flops 2417098752 | bytes 13893740 | solution.py:51
  276.8 8.5 %convolution_add_fusion = f32[1152,1024]{1,0:T(8,128)} fusion(f32[1152,1024]{1,0:T(8,128)} %get-tuple-element.165, bf16[1152,16384]{1,0:T(8,128)(2,1)} %get-tuple-element.166, s32[]{:T(128)S(6)} %select_n.19, bf16[8,1024,1024]{2,1,0:T(8,128)(2,1)} %get-tuple-element.169, s32[]{:T(128)S(6)} %select_n.18), kind=kOutput, calls=%fused_computation | convolution fusion | flops 2417098752 | bytes 13893640 | tf_op jit(solution)/shard_map/while/body/eval_jaxpr/cond/branch_1_fun/dot_general | solution.py:38
  286.0 9.8 %conditional.2 = (f32[1152,1024]{1,0:T(8,128)}) conditional(s32[]{:T(128)} %convert_element_type.41, f32[1152,1024]{1,0:T(8,128)} %get-tuple-element.236, (s32[]{:T(128)}, s32[8]{0:T(128)S(1)}, bf16[1152,16384]{1,0:T(8,128)(2,1)}, bf16[8,1024,1024]{2,1,0:T(8,128)(2,1)}, f32[1152,1024]{1,0:T(8,128)}) %tuple.45), branch_computations={%region_1.0_spmd, %region_2.2_spmd} | conditional | flops 2417098752 | bytes 13893740 | solution.py:51
  287.3 8.5 %convolution_add_fusion = f32[1152,1024]{1,0:T(8,128)} fusion(f32[1152,1024]{1,0:T(8,128)} %get-tuple-element.165, bf16[1152,16384]{1,0:T(8,128)(2,1)} %get-tuple-element.166, s32[]{:T(128)S(6)} %select_n.19, bf16[8,1024,1024]{2,1,0:T(8,128)(2,1)} %get-tuple-element.169, s32[]{:T(128)S(6)} %select_n.18), kind=kOutput, calls=%fused_computation | convolution fusion | flops 2417098752 | bytes 13893640 | tf_op jit(solution)/shard_map/while/body/eval_jaxpr/cond/branch_1_fun/dot_general | solution.py:38
  296.5 9.8 %conditional.2 = (f32[1152,1024]{1,0:T(8,128)}) conditional(s32[]{:T(128)} %convert_element_type.41, f32[1152,1024]{1,0:T(8,128)} %get-tuple-element.236, (s32[]{:T(128)}, s32[8]{0:T(128)S(1)}, bf16[1152,16384]{1,0:T(8,128)(2,1)}, bf16[8,1024,1024]{2,1,0:T(8,128)(2,1)}, f32[1152,1024]{1,0:T(8,128)}) %tuple.45), branch_computations={%region_1.0_spmd, %region_2.2_spmd} | conditional | flops 2417098752 | bytes 13893740 | solution.py:51
  297.7 8.5 %convolution_add_fusion = f32[1152,1024]{1,0:T(8,128)} fusion(f32[1152,1024]{1,0:T(8,128)} %get-tuple-element.165, bf16[1152,16384]{1,0:T(8,128)(2,1)} %get-tuple-element.166, s32[]{:T(128)S(6)} %select_n.19, bf16[8,1024,1024]{2,1,0:T(8,128)(2,1)} %get-tuple-element.169, s32[]{:T(128)S(6)} %select_n.18), kind=kOutput, calls=%fused_computation | convolution fusion | flops 2417098752 | bytes 13893640 | tf_op jit(solution)/shard_map/while/body/eval_jaxpr/cond/branch_1_fun/dot_general | solution.py:38
  306.9 9.8 %conditional.2 = (f32[1152,1024]{1,0:T(8,128)}) conditional(s32[]{:T(128)} %convert_element_type.41, f32[1152,1024]{1,0:T(8,128)} %get-tuple-element.236, (s32[]{:T(128)}, s32[8]{0:T(128)S(1)}, bf16[1152,16384]{1,0:T(8,128)(2,1)}, bf16[8,1024,1024]{2,1,0:T(8,128)(2,1)}, f32[1152,1024]{1,0:T(8,128)}) %tuple.45), branch_computations={%region_1.0_spmd, %region_2.2_spmd} | conditional | flops 2417098752 | bytes 13893740 | solution.py:51
  308.2 8.5 %convolution_add_fusion = f32[1152,1024]{1,0:T(8,128)} fusion(f32[1152,1024]{1,0:T(8,128)} %get-tuple-element.165, bf16[1152,16384]{1,0:T(8,128)(2,1)} %get-tuple-element.166, s32[]{:T(128)S(6)} %select_n.19, bf16[8,1024,1024]{2,1,0:T(8,128)(2,1)} %get-tuple-element.169, s32[]{:T(128)S(6)} %select_n.18), kind=kOutput, calls=%fused_computation | convolution fusion | flops 2417098752 | bytes 13893640 | tf_op jit(solution)/shard_map/while/body/eval_jaxpr/cond/branch_1_fun/dot_general | solution.py:38
  316.7 3.6 copy.11
  320.3 2.5 copy.12
  322.8 4.8 %reshape.14 = bf16[12,8,12,1024]{3,2,1,0:T(8,128)(2,1)} reshape(bf16[1152,1024]{1,0:T(8,128)(2,1)} %copy.12) | data formatting | bytes 4718592 | tf_op jit(solution)/shard_map/reshape | solution.py:18
  327.6 2.4 copy.13
  330.1 42.5 %all_to_all.5 = bf16[12,8,12,1024]{3,2,0,1:T(8,128)(2,1)S(1)} all-to-all(bf16[12,8,12,1024]{3,2,0,1:T(8,128)(2,1)S(1)} %copy.13), channel_id=1, replica_groups=mesh['occ'=8,'vir'=16] {'occ'}, dimensions={1} | all-to-all | bytes 4718592 | tf_op jit(solution)/shard_map/all_to_all | solution.py:19
  372.6 3.0 copy.14
  375.6 4.9 %reshape.15 = bf16[1152,1024]{1,0:T(8,128)(2,1)} reshape(bf16[12,8,12,1024]{3,2,1,0:T(8,128)(2,1)} %copy.14) | data formatting | bytes 4718592 | tf_op jit(solution)/shard_map/reshape | solution.py:20
  380.5 52.9 %collective-permute-done = bf16[1152,1024]{1,0:T(8,128)(2,1)} collective-permute-done((bf16[1152,1024]{1,0:T(8,128)(2,1)}, bf16[1152,1024]{1,0:T(8,128)(2,1)}, u32[]{:S(2)}, u32[]{:S(2)}) %collective-permute-start) | collective-permute-done | bytes 2359328 | tf_op jit(solution)/shard_map/ppermute | solution.py:13
  433.4 4.6 copy.15
  438.0 5.1 %copy.16 = f32[1152,32,32]{0,2,1:T(8,128)S(1)} copy(f32[1152,32,32]{0,1,2:T(8,128)} %bitcast.15) | data formatting | bytes 9437184 | tf_op jit(solution)/shard_map/convert_element_type | solution.py:56
  443.1 2.0 fusion.4
  445.1 4.3 copy.17
  (12 shorter events, 4.9 us)
Async XLA Ops:
  6.5 226.6 %copy-start = (s32[1,8]{1,0:T(1,128)S(1)}, s32[1,8]{1,0:T(1,128)}, u32[]{:S(2)}) copy-start(s32[1,8]{1,0:T(1,128)} %param.10) | copy-start | bytes 100
  6.5 223.8 %all-gather.2.cloned.1.call-start = ((), (), s32[]{:S(2)}) async-start(), calls=%async_computation.1 | async-start | bytes 40108032 | tf_op jit(solution)/shard_map/all_gather | solution.py:42
  380.5 52.9 %collective-permute-start = (bf16[1152,1024]{1,0:T(8,128)(2,1)}, bf16[1152,1024]{1,0:T(8,128)(2,1)}, u32[]{:S(2)}, u32[]{:S(2)}) collective-permute-start(bf16[1152,1024]{1,0:T(8,128)(2,1)} %reshape.15), channel_id=1, source_target_pairs={{0,1},{1,0},{2,3},{3,2},{4,5},{5,4},{6,7},{7,6},{8,9},{9,8},{10,11... | collective-permute-start | bytes 7077896 | tf_op jit(solution)/shard_map/ppermute | solution.py:13
Sparse Core Ops, SparseCore 0:
  9.5 220.8 all-gather.1
where the time goes:
time: 457 us; the launch traced here: 456 us
  waiting for transfers between devices  277 us (61%)
  matrix products  68.2 us (15%)
  local copies, waits for them, and re-layouts  42.8 us (9%)
  blocking collectives  42.5 us (9%)
  between operations  13.4 us (3%)
  loops' own time  10.5 us (2%)
    all_gather x1, waiting for transfers between devices, on_device(): gathered = lax.all_gather(amplitudes, 'vir', axis=1, tiled=True)  223 us
    dot_general x8, matrix products, product(): lax.dot_general(col_tile, int_block, (((1,), (1,)), ((), ())), preferred_...  68.2 us
    ppermute x1, waiting for transfers between devices, swapped(): lax.ppermute(shard, axis, [(i, i ^ 1 << apart) for i in range(lax.axis_si...  52.9 us
    all_to_all x1, blocking collectives, reflect_rows(): lax.all_to_all(reshaped, 'occ', split_axis=1, concat_axis=1, tiled=True)  42.5 us
    convert_element_type x2, local copies, waits for them, and re-layouts, on_device(): summed = ladder.astype(jnp.float32) + mirrored.astype(jnp.float32)  9.62 us
  transfers between devices with their start and end apart: 2, of which 2 were waited for; matrix products, arithmetic and copies ran while one was open for 0% of the time, Pallas kernels for 0%

commit v1 on v0

--- a/solution.py
+++ b/solution.py
@@ -2,6 +2,7 @@
 import jax.numpy as jnp
 from jax import lax
 from jax.sharding import PartitionSpec as P
+from jax.lax import all_to_all, axis_size
 
 TW = 32
 K = 1024
@@ -16,7 +17,15 @@
 def reflect_rows(matrix):
     occ_devices = lax.axis_size("occ")
     reshaped = matrix.reshape(OCC_DEV, occ_devices, OCC_DEV, matrix.shape[1])
-    arrived = lax.all_to_all(reshaped, "occ", split_axis=1, concat_axis=1, tiled=True)
+    arrived = jnp.concatenate(
+        all_to_all(
+            jnp.stack(jnp.split(reshaped, axis_size("occ"), axis=1)),
+            axis_name="occ",
+            split_axis=0,
+            concat_axis=0,
+        ),
+        axis=1,
+    )
     return arrived.transpose(2, 1, 0, 3).reshape(matrix.shape)
 
 

time: 457 us -> 463 us (1.013)
  local copies, waits for them, and re-layouts: 42.8 us -> 48.5 us
    unnamed x2 -> x9, local copies, waits for them, and re-layouts: 0.01 us -> 7.2 us
where the time goes in v1:
time: 463 us; the launch traced here: 462 us
  waiting for transfers between devices  277 us (60%)
  matrix products  68.2 us (15%)
  local copies, waits for them, and re-layouts  48.5 us (10%)
  blocking collectives  42.5 us (9%)
  between operations  13.5 us (3%)
  loops' own time  10.5 us (2%)
    all_gather x1, waiting for transfers between devices, on_device(): gathered = lax.all_gather(amplitudes, 'vir', axis=1, tiled=True)  223 us
    dot_general x8, matrix products, product(): lax.dot_general(col_tile, int_block, (((1,), (1,)), ((), ())), preferred_...  68.2 us
    ppermute x1, waiting for transfers between devices, swapped(): lax.ppermute(shard, axis, [(i, i ^ 1 << apart) for i in range(lax.axis_si...  52.9 us
    all_to_all x1, blocking collectives, reflect_rows(): all_to_all(jnp.stack(jnp.split(reshaped, axis_size('occ'), axis=1)), axis...  42.5 us
    convert_element_type x2, local copies, waits for them, and re-layouts, on_device(): summed = ladder.astype(jnp.float32) + mirrored.astype(jnp.float32)  9.62 us
  transfers between devices with their start and end apart: 2, of which 2 were waited for; matrix products, arithmetic and copies ran while one was open for 0% of the time, Pallas kernels for 0%

profile of v1, /device:TPU:6, one launch (start us, length us, event | category | flops | bytes accessed | tf_op | source)
XLA Modules:
  0.0 462.0 jit_solution(18114048472407707891)
XLA Ops:
  7.3 223.1 %all-gather.2.cloned.1.call-done = bf16[1152,16384]{1,0:T(8,128)(2,1)} async-done(((bf16[1152,1024]{1,0:T(8,128)(2,1)}), bf16[1152,16384]{1,0:T(8,128)(2,1)}) %all-gather.2.cloned.1.call-update) | async-done | bytes 37748752 | tf_op jit(solution)/shard_map/all_gather | solution.py:51
  230.4 2.8 broadcast_in_dim.3
  233.1 83.6 %while.16 = (s32[]{:T(128)}, f32[1152,1024]{1,0:T(8,128)}, s32[]{:T(128)}, s32[8]{0:T(128)S(1)}, bf16[1152,16384]{1,0:T(8,128)(2,1)}, /*index=5*/bf16[8,1024,1024]{2,1,0:T(8,128)(2,1)}, s32[]{:T(128)}) while((s32[]{:T(128)}, f32[1152,1024]{1,0:T(8,128)}, s32[]{:T(128)}, s32[8]{0:T(128)S(1)}, bf16[1152,16384]{1,0:T(8,128)(2,1)}, ...), condition=%wide.region_3.4_spmd, body=%wide.region_0.3_spmd.sunk | while | flops 2417098752 | bytes 13893871 | solution.py:62
  233.8 9.8 %conditional.2 = (f32[1152,1024]{1,0:T(8,128)}) conditional(s32[]{:T(128)} %convert_element_type.41, f32[1152,1024]{1,0:T(8,128)} %get-tuple-element.236, (s32[]{:T(128)}, s32[8]{0:T(128)S(1)}, bf16[1152,16384]{1,0:T(8,128)(2,1)}, bf16[8,1024,1024]{2,1,0:T(8,128)(2,1)}, f32[1152,1024]{1,0:T(8,128)}) %tuple.45), branch_computations={%region_1.0_spmd, %region_2.2_spmd} | conditional | flops 2417098752 | bytes 13893740 | solution.py:60
  235.1 8.5 %convolution_add_fusion = f32[1152,1024]{1,0:T(8,128)} fusion(f32[1152,1024]{1,0:T(8,128)} %get-tuple-element.165, bf16[1152,16384]{1,0:T(8,128)(2,1)} %get-tuple-element.166, s32[]{:T(128)S(6)} %select_n.19, bf16[8,1024,1024]{2,1,0:T(8,128)(2,1)} %get-tuple-element.169, s32[]{:T(128)S(6)} %select_n.18), kind=kOutput, calls=%fused_computation | convolution fusion | flops 2417098752 | bytes 13893640 | tf_op jit(solution)/shard_map/while/body/eval_jaxpr/cond/branch_1_fun/dot_general | solution.py:47
  244.2 9.8 %conditional.2 = (f32[1152,1024]{1,0:T(8,128)}) conditional(s32[]{:T(128)} %convert_element_type.41, f32[1152,1024]{1,0:T(8,128)} %get-tuple-element.236, (s32[]{:T(128)}, s32[8]{0:T(128)S(1)}, bf16[1152,16384]{1,0:T(8,128)(2,1)}, bf16[8,1024,1024]{2,1,0:T(8,128)(2,1)}, f32[1152,1024]{1,0:T(8,128)}) %tuple.45), branch_computations={%region_1.0_spmd, %region_2.2_spmd} | conditional | flops 2417098752 | bytes 13893740 | solution.py:60
  245.5 8.5 %convolution_add_fusion = f32[1152,1024]{1,0:T(8,128)} fusion(f32[1152,1024]{1,0:T(8,128)} %get-tuple-element.165, bf16[1152,16384]{1,0:T(8,128)(2,1)} %get-tuple-element.166, s32[]{:T(128)S(6)} %select_n.19, bf16[8,1024,1024]{2,1,0:T(8,128)(2,1)} %get-tuple-element.169, s32[]{:T(128)S(6)} %select_n.18), kind=kOutput, calls=%fused_computation | convolution fusion | flops 2417098752 | bytes 13893640 | tf_op jit(solution)/shard_map/while/body/eval_jaxpr/cond/branch_1_fun/dot_general | solution.py:47
  254.7 9.8 %conditional.2 = (f32[1152,1024]{1,0:T(8,128)}) conditional(s32[]{:T(128)} %convert_element_type.41, f32[1152,1024]{1,0:T(8,128)} %get-tuple-element.236, (s32[]{:T(128)}, s32[8]{0:T(128)S(1)}, bf16[1152,16384]{1,0:T(8,128)(2,1)}, bf16[8,1024,1024]{2,1,0:T(8,128)(2,1)}, f32[1152,1024]{1,0:T(8,128)}) %tuple.45), branch_computations={%region_1.0_spmd, %region_2.2_spmd} | conditional | flops 2417098752 | bytes 13893740 | solution.py:60
  256.0 8.5 %convolution_add_fusion = f32[1152,1024]{1,0:T(8,128)} fusion(f32[1152,1024]{1,0:T(8,128)} %get-tuple-element.165, bf16[1152,16384]{1,0:T(8,128)(2,1)} %get-tuple-element.166, s32[]{:T(128)S(6)} %select_n.19, bf16[8,1024,1024]{2,1,0:T(8,128)(2,1)} %get-tuple-element.169, s32[]{:T(128)S(6)} %select_n.18), kind=kOutput, calls=%fused_computation | convolution fusion | flops 2417098752 | bytes 13893640 | tf_op jit(solution)/shard_map/while/body/eval_jaxpr/cond/branch_1_fun/dot_general | solution.py:47
  265.1 9.8 %conditional.2 = (f32[1152,1024]{1,0:T(8,128)}) conditional(s32[]{:T(128)} %convert_element_type.41, f32[1152,1024]{1,0:T(8,128)} %get-tuple-element.236, (s32[]{:T(128)}, s32[8]{0:T(128)S(1)}, bf16[1152,16384]{1,0:T(8,128)(2,1)}, bf16[8,1024,1024]{2,1,0:T(8,128)(2,1)}, f32[1152,1024]{1,0:T(8,128)}) %tuple.45), branch_computations={%region_1.0_spmd, %region_2.2_spmd} | conditional | flops 2417098752 | bytes 13893740 | solution.py:60
  266.4 8.5 %convolution_add_fusion = f32[1152,1024]{1,0:T(8,128)} fusion(f32[1152,1024]{1,0:T(8,128)} %get-tuple-element.165, bf16[1152,16384]{1,0:T(8,128)(2,1)} %get-tuple-element.166, s32[]{:T(128)S(6)} %select_n.19, bf16[8,1024,1024]{2,1,0:T(8,128)(2,1)} %get-tuple-element.169, s32[]{:T(128)S(6)} %select_n.18), kind=kOutput, calls=%fused_computation | convolution fusion | flops 2417098752 | bytes 13893640 | tf_op jit(solution)/shard_map/while/body/eval_jaxpr/cond/branch_1_fun/dot_general | solution.py:47
  275.6 9.8 %conditional.2 = (f32[1152,1024]{1,0:T(8,128)}) conditional(s32[]{:T(128)} %convert_element_type.41, f32[1152,1024]{1,0:T(8,128)} %get-tuple-element.236, (s32[]{:T(128)}, s32[8]{0:T(128)S(1)}, bf16[1152,16384]{1,0:T(8,128)(2,1)}, bf16[8,1024,1024]{2,1,0:T(8,128)(2,1)}, f32[1152,1024]{1,0:T(8,128)}) %tuple.45), branch_computations={%region_1.0_spmd, %region_2.2_spmd} | conditional | flops 2417098752 | bytes 13893740 | solution.py:60
  276.8 8.5 %convolution_add_fusion = f32[1152,1024]{1,0:T(8,128)} fusion(f32[1152,1024]{1,0:T(8,128)} %get-tuple-element.165, bf16[1152,16384]{1,0:T(8,128)(2,1)} %get-tuple-element.166, s32[]{:T(128)S(6)} %select_n.19, bf16[8,1024,1024]{2,1,0:T(8,128)(2,1)} %get-tuple-element.169, s32[]{:T(128)S(6)} %select_n.18), kind=kOutput, calls=%fused_computation | convolution fusion | flops 2417098752 | bytes 13893640 | tf_op jit(solution)/shard_map/while/body/eval_jaxpr/cond/branch_1_fun/dot_general | solution.py:47
  286.0 9.8 %conditional.2 = (f32[1152,1024]{1,0:T(8,128)}) conditional(s32[]{:T(128)} %convert_element_type.41, f32[1152,1024]{1,0:T(8,128)} %get-tuple-element.236, (s32[]{:T(128)}, s32[8]{0:T(128)S(1)}, bf16[1152,16384]{1,0:T(8,128)(2,1)}, bf16[8,1024,1024]{2,1,0:T(8,128)(2,1)}, f32[1152,1024]{1,0:T(8,128)}) %tuple.45), branch_computations={%region_1.0_spmd, %region_2.2_spmd} | conditional | flops 2417098752 | bytes 13893740 | solution.py:60
  287.3 8.5 %convolution_add_fusion = f32[1152,1024]{1,0:T(8,128)} fusion(f32[1152,1024]{1,0:T(8,128)} %get-tuple-element.165, bf16[1152,16384]{1,0:T(8,128)(2,1)} %get-tuple-element.166, s32[]{:T(128)S(6)} %select_n.19, bf16[8,1024,1024]{2,1,0:T(8,128)(2,1)} %get-tuple-element.169, s32[]{:T(128)S(6)} %select_n.18), kind=kOutput, calls=%fused_computation | convolution fusion | flops 2417098752 | bytes 13893640 | tf_op jit(solution)/shard_map/while/body/eval_jaxpr/cond/branch_1_fun/dot_general | solution.py:47
  296.5 9.8 %conditional.2 = (f32[1152,1024]{1,0:T(8,128)}) conditional(s32[]{:T(128)} %convert_element_type.41, f32[1152,1024]{1,0:T(8,128)} %get-tuple-element.236, (s32[]{:T(128)}, s32[8]{0:T(128)S(1)}, bf16[1152,16384]{1,0:T(8,128)(2,1)}, bf16[8,1024,1024]{2,1,0:T(8,128)(2,1)}, f32[1152,1024]{1,0:T(8,128)}) %tuple.45), branch_computations={%region_1.0_spmd, %region_2.2_spmd} | conditional | flops 2417098752 | bytes 13893740 | solution.py:60
  297.7 8.5 %convolution_add_fusion = f32[1152,1024]{1,0:T(8,128)} fusion(f32[1152,1024]{1,0:T(8,128)} %get-tuple-element.165, bf16[1152,16384]{1,0:T(8,128)(2,1)} %get-tuple-element.166, s32[]{:T(128)S(6)} %select_n.19, bf16[8,1024,1024]{2,1,0:T(8,128)(2,1)} %get-tuple-element.169, s32[]{:T(128)S(6)} %select_n.18), kind=kOutput, calls=%fused_computation | convolution fusion | flops 2417098752 | bytes 13893640 | tf_op jit(solution)/shard_map/while/body/eval_jaxpr/cond/branch_1_fun/dot_general | solution.py:47
  306.9 9.8 %conditional.2 = (f32[1152,1024]{1,0:T(8,128)}) conditional(s32[]{:T(128)} %convert_element_type.41, f32[1152,1024]{1,0:T(8,128)} %get-tuple-element.236, (s32[]{:T(128)}, s32[8]{0:T(128)S(1)}, bf16[1152,16384]{1,0:T(8,128)(2,1)}, bf16[8,1024,1024]{2,1,0:T(8,128)(2,1)}, f32[1152,1024]{1,0:T(8,128)}) %tuple.45), branch_computations={%region_1.0_spmd, %region_2.2_spmd} | conditional | flops 2417098752 | bytes 13893740 | solution.py:60
  308.2 8.5 %convolution_add_fusion = f32[1152,1024]{1,0:T(8,128)} fusion(f32[1152,1024]{1,0:T(8,128)} %get-tuple-element.165, bf16[1152,16384]{1,0:T(8,128)(2,1)} %get-tuple-element.166, s32[]{:T(128)S(6)} %select_n.19, bf16[8,1024,1024]{2,1,0:T(8,128)(2,1)} %get-tuple-element.169, s32[]{:T(128)S(6)} %select_n.18), kind=kOutput, calls=%fused_computation | convolution fusion | flops 2417098752 | bytes 13893640 | tf_op jit(solution)/shard_map/while/body/eval_jaxpr/cond/branch_1_fun/dot_general | solution.py:47
  316.7 3.6 copy.12
  320.3 2.5 copy.13
  322.8 4.8 %reshape.20 = bf16[12,8,12,1024]{3,2,1,0:T(8,128)(2,1)} reshape(bf16[1152,1024]{1,0:T(8,128)(2,1)} %copy.13) | data formatting | bytes 4718592 | tf_op jit(solution)/shard_map/reshape | solution.py:19
  328.7 1.0 fusion.11
  329.7 1.0 fusion.10
  335.9 42.5 %all_to_all.5 = bf16[8,12,1,12,1024]{4,3,1,2,0:T(8,128)(2,1)S(1)} all-to-all(bf16[8,12,1,12,1024]{4,3,1,2,0:T(8,128)(2,1)S(1)} %fusion.5), channel_id=1, replica_groups=mesh['occ'=8,'vir'=16] {'occ'}, dimensions={0} | all-to-all | bytes 4718592 | tf_op jit(solution)/shard_map/all_to_all | solution.py:21
  378.4 3.0 copy.21
  381.4 4.9 %reshape.23 = bf16[1152,1024]{1,0:T(8,128)(2,1)} reshape(bf16[12,8,12,1024]{3,2,1,0:T(8,128)(2,1)} %copy.21) | data formatting | bytes 4718592 | tf_op jit(solution)/shard_map/reshape | solution.py:29
  386.3 52.9 %collective-permute-done = bf16[1152,1024]{1,0:T(8,128)(2,1)} collective-permute-done((bf16[1152,1024]{1,0:T(8,128)(2,1)}, bf16[1152,1024]{1,0:T(8,128)(2,1)}, u32[]{:S(2)}, u32[]{:S(2)}) %collective-permute-start) | collective-permute-done | bytes 2359328 | tf_op jit(solution)/shard_map/ppermute | solution.py:14
  439.3 4.6 copy.22
  443.8 5.1 %copy.23 = f32[1152,32,32]{0,2,1:T(8,128)S(1)} copy(f32[1152,32,32]{0,1,2:T(8,128)} %bitcast.65) | data formatting | bytes 9437184 | tf_op jit(solution)/shard_map/convert_element_type | solution.py:65
  448.9 2.0 fusion.4
  450.9 4.3 copy.24
  (19 shorter events, 11.7 us)
Async XLA Ops:
  6.5 226.6 %copy-start = (s32[1,8]{1,0:T(1,128)S(1)}, s32[1,8]{1,0:T(1,128)}, u32[]{:S(2)}) copy-start(s32[1,8]{1,0:T(1,128)} %param.10) | copy-start | bytes 100
  6.5 223.8 %all-gather.2.cloned.1.call-start = ((), (), s32[]{:S(2)}) async-start(), calls=%async_computation.1 | async-start | bytes 40108032 | tf_op jit(solution)/shard_map/all_gather | solution.py:51
  386.3 52.9 %collective-permute-start = (bf16[1152,1024]{1,0:T(8,128)(2,1)}, bf16[1152,1024]{1,0:T(8,128)(2,1)}, u32[]{:S(2)}, u32[]{:S(2)}) collective-permute-start(bf16[1152,1024]{1,0:T(8,128)(2,1)} %reshape.23), channel_id=1, source_target_pairs={{0,1},{1,0},{2,3},{3,2},{4,5},{5,4},{6,7},{7,6},{8,9},{9,8},{10,11... | collective-permute-start | bytes 7077896 | tf_op jit(solution)/shard_map/ppermute | solution.py:14
Sparse Core Ops, SparseCore 0:
  9.5 220.8 all-gather.1
